TPU v7x, 32 devices: a whole 2x2x4 slice. The times are simulated.
32 devices in a mesh: freq: 4 (over y, x), bond: 8 (over z, core).
Axes of the slice: x: 2, y: 2, z: 4, core: 2. Of those that a mesh axis runs over, the one named last changes fastest.
Arguments:
- gamma: bfloat16 [2, 8, 32, 384, 384], P(None, 'freq', 'bond'), may hold values from -1 to 1
- green: float32 [2, 8, 32, 256], P(None, 'freq', 'bond'), may hold values from -6 to 6
- single: float32 [2, 8, 32, 256], P(None, 'freq', 'bond'), may hold values from -6 to 6
- bond_site: int32 [384], replicated, may hold values from 0 to 255
- causal_mask: int32 [8, 3, 3], P('freq'), may hold values 0 or 1
- site_perm: int32 [384], replicated, may hold values from 0 to 383, each once
Outputs:
- p_vertex: bfloat16 [2, 8, 384, 32, 384], P(None, 'freq', 'bond')
Inputs may be any that keep to these rules, and one draw needn't show every extreme that they name: `bond_site`: each of the 384 bond-Keldysh indices names one site. `causal_mask`: 1 keeps a causality block of 128 x 128 entries, 0 removes it. `site_perm`: a permutation of the 384 column indices.
All inputs are finite; a program needn't handle non-finite values.
Results may differ from a plain program's by a relative error of at most 0.0049.
Values may be sent and summed in bfloat16 or wider, within the bound.
A program may use at most 128 MiB of HBM per device.

v0:
```python
import math

import jax
import jax.numpy as jnp
from jax import lax
from jax.sharding import PartitionSpec as P


def times_complex(first_real, first_imag, second_real, second_imag):
    return (
        first_real * second_real - first_imag * second_imag,
        first_real * second_imag + first_imag * second_real,
    )


def products(pattern, left, right):
    return jnp.einsum(pattern, left, right, preferred_element_type=jnp.float32)


def complex_flow(pattern, left_real, left_imag, gamma_real, gamma_imag):
    flow_real = products(pattern, left_real, gamma_real) - products(pattern, left_imag, gamma_imag)
    flow_imag = products(pattern, left_real, gamma_imag) + products(pattern, left_imag, gamma_real)
    return (flow_real, flow_imag)


def compute_flows(gamma_part, bubble_part, mask_part, site_perm):
    order = gamma_part.shape[-1]
    blocks = mask_part.shape[-1]
    width = order // blocks
    gamma_real = gamma_part[0].astype(jnp.float32)
    gamma_imag = gamma_part[1].astype(jnp.float32)
    bubble_real = bubble_part[0][:, :, None, :]
    bubble_imag = bubble_part[1][:, :, None, :]
    left_real = (gamma_real * bubble_real - gamma_imag * bubble_imag).astype(jnp.bfloat16)
    left_imag = (gamma_real * bubble_imag + gamma_imag * bubble_real).astype(jnp.bfloat16)
    flow_real, flow_imag = complex_flow(
        "wsrk,wskc->wrsc", left_real, left_imag, gamma_part[0], gamma_part[1]
    )
    spread = jnp.repeat(jnp.repeat(mask_part, width, axis=1), width, axis=2).astype(jnp.float32)
    flow_real = flow_real * spread[:, :, None, :]
    flow_imag = flow_imag * spread[:, :, None, :]
    rounded = jnp.stack([flow_real, flow_imag]).astype(jnp.bfloat16)
    return jnp.take(rounded, site_perm, axis=4)


def body(gamma, green, single, bond_site, causal_mask, site_perm):
    local = green.shape[1]
    count = local * lax.axis_size("freq")
    whole_green, whole_single = (
        lax.all_gather(green, "freq", axis=1, tiled=True),
        lax.all_gather(single, "freq", axis=1, tiled=True),
    )
    green_bond = jnp.take(whole_green, bond_site, axis=3)
    single_bond = jnp.take(whole_single, bond_site, axis=3)
    owned = lax.axis_index("freq") * local + jnp.arange(local, dtype=jnp.int32)
    shifts = (jnp.arange(count, dtype=jnp.int32)[None, :] + owned[:, None]) % count
    green_moved = jnp.take(green_bond, shifts, axis=1)
    single_moved = jnp.take(single_bond, shifts, axis=1)
    first = times_complex(
        green_bond[0][None], green_bond[1][None], single_moved[0], single_moved[1]
    )
    second = times_complex(
        single_bond[0][None], single_bond[1][None], green_moved[0], green_moved[1]
    )
    factor = 1.0 / math.sqrt(count)
    bubble = jnp.stack(
        [
            jnp.sum(first[0] + second[0], axis=1) * factor,
            jnp.sum(first[1] + second[1], axis=1) * factor,
        ]
    )
    flows = compute_flows(gamma, bubble, causal_mask, site_perm)
    return lax.all_to_all(flows, "bond", split_axis=2, concat_axis=3, tiled=True)


def solution(mesh):
    in_specs = (
        P(None, "freq", "bond", None, None),
        P(None, "freq", "bond", None),
        P(None, "freq", "bond", None),
        P(),
        P("freq", None, None),
        P(),
    )
    out_specs = P(None, "freq", "bond", None, None)
    return jax.shard_map(body, mesh=mesh, in_specs=in_specs, out_specs=out_specs, check_vma=False)
```

profile of v0, /device:TPU:0, one launch (start us, length us, event | category | flops | bytes accessed | tf_op | source)
XLA Modules:
  0.0 229.6 jit_solution(18322149337392258693)
XLA Ops:
  2.3 9.7 %all_gather.6 = f32[2,8,4,256]{3,2,0,1:T(4,128)S(1)} all-gather(f32[2,2,4,256]{3,2,0,1:T(4,128)S(1)} %copy.95), channel_id=1, replica_groups=mesh['freq'=4,'bond'=8] {'freq'}, dimensions={1}, use_global_device_ids=true | all-gather | bytes 81920 | tf_op jit(solution)/shard_map/all_gather | solution.py:50
  13.1 8.2 %all_gather.7 = f32[2,8,4,256]{3,2,0,1:T(4,128)S(1)} all-gather(f32[2,2,4,256]{3,2,0,1:T(4,128)S(1)} %copy.98), channel_id=1, replica_groups=mesh['freq'=4,'bond'=8] {'freq'}, dimensions={1}, use_global_device_ids=true | all-gather | bytes 81920 | tf_op jit(solution)/shard_map/all_gather | solution.py:51
  21.7 3.1 %gather_fusion.1 = f32[384,2,8,4]{2,3,1,0:T(4,128)} fusion(f32[2,8,4,256]{1,2,3,0:T(4,128)S(1)} %copy.96, s32[1024]{0:T(1024)S(1)} %pad_clamp_fusion.2), kind=kCustom, calls=%fused_computation.clone | custom fusion | bytes 198144 | tf_op jit(solution)/shard_map/jit(_take)/gather | solution.py:53
  24.8 3.1 %gather_fusion.2 = f32[384,2,8,4]{2,3,1,0:T(4,128)} fusion(f32[2,8,4,256]{1,2,3,0:T(4,128)S(1)} %copy.99, s32[1024]{0:T(1024)S(1)} %pad_clamp_fusion.2), kind=kCustom, calls=%fused_computation.2.clone | custom fusion | bytes 198144 | tf_op jit(solution)/shard_map/jit(_take)/gather | solution.py:54
  28.0 2.8 %select_bitcast_fusion.2 = (f32[2,8,4,384]{1,2,0,3:T(4,128)S(1)}, f32[2,8,4,384]{1,2,0,3:T(4,128)S(1)}) fusion(f32[384,2,8,4]{2,3,1,0:T(4,128)} %gather_fusion.1, pred[384]{0:T(512)(128)(4,1)S(1)} %compare_and_fusion.1, f32[384,2,8,4]{2,3,1,0:T(4,128)} %gather_fusion.2), kind=kLoop, calls=%fused_computation.40 | loop fusion | flops 49152 | bytes 393600 | tf_op jit(solution)/shard_map/jit(_take)/select_n | solution.py:53
  31.5 1.0 copy.104
  32.5 2.0 slice_bitcast_fusion.1
  35.9 1.4 copy.102
  37.3 1.4 copy.103
  38.7 1.4 copy.106
  40.0 1.4 copy.97
  41.7 7.0 %fusion.6 = f32[2,4,384,384]{3,2,1,0:T(8,128)} fusion(f32[2,4,384]{2,1,0:T(4,128)S(1)} %copy_multiply_fusion, f32[2,4,384]{2,1,0:T(4,128)S(1)} %copy_multiply_fusion.1, bf16[2,2,4,384,384]{4,3,2,1,0:T(8,128)(2,1)} %param.10), kind=kOutput, calls=%fused_computation.18 | convolution fusion | flops 913047552 | bytes 11821056 | tf_op jit(solution)/shard_map/wsrk,wskc->wrsc/dot_general | solution.py:17
  48.7 3.8 %fusion.4 = f32[2,4,384,384]{3,2,1,0:T(8,128)} fusion(f32[2,4,384]{2,1,0:T(4,128)S(1)} %copy_multiply_fusion, f32[2,4,384]{2,1,0:T(4,128)S(1)} %copy_multiply_fusion.1, bf16[2,2,4,384,384]{4,3,2,1,0:T(8,128)(2,1)S(1)} %bitcast.115), kind=kOutput, calls=%fused_computation.17 | convolution fusion | flops 913047552 | bytes 11821056 | tf_op jit(solution)/shard_map/wsrk,wskc->wrsc/dot_general | solution.py:17
  53.2 6.1 %fusion.12 = bf16[1,2,384,4,384]{4,2,3,1,0:T(8,128)(2,1)S(1)} fusion(f32[2,4,384,384]{3,2,1,0:T(8,128)} %fusion.6, f32[2,384,384]{2,1,0:T(8,128)S(1)} %copy.111, f32[2,4,384]{2,1,0:T(4,128)S(1)} %copy_multiply_fusion, f32[2,4,384]{2,1,0:T(4,128)S(1)} %copy_multiply_fusion.1, bf16[2,2,4,384,384]{4,3,2,1,0:T(8,128)(2,1)} %param.10), kind=kOutput, calls=%fused_computation.21 | convolution fusion | flops 916586496 | bytes 15360000 | tf_op jit(solution)/shard_map/wsrk,wskc->wrsc/dot_general | solution.py:17
  59.3 6.1 %fusion.13 = bf16[1,2,384,4,384]{4,2,3,1,0:T(8,128)(2,1)S(1)} fusion(f32[2,4,384,384]{3,2,1,0:T(8,128)} %fusion.4, f32[2,384,384]{2,1,0:T(8,128)S(1)} %copy.111, f32[2,4,384]{2,1,0:T(4,128)S(1)} %copy_multiply_fusion, f32[2,4,384]{2,1,0:T(4,128)S(1)} %copy_multiply_fusion.1, bf16[2,2,4,384,384]{4,3,2,1,0:T(8,128)(2,1)} %param.10), kind=kOutput, calls=%fused_computation.22 | convolution fusion | flops 916586496 | bytes 15360000 | tf_op jit(solution)/shard_map/wsrk,wskc->wrsc/dot_general | solution.py:17
  65.4 2.7 %pad_maximum_fusion = bf16[2,2,384,4,384]{4,2,3,1,0:T(8,128)(2,1)} fusion(bf16[1,2,384,4,384]{4,2,3,1,0:T(8,128)(2,1)S(1)} %fusion.13, bf16[1,2,384,4,384]{4,2,3,1,0:T(8,128)(2,1)S(1)} %fusion.12), kind=kLoop, calls=%fused_computation.13 | loop fusion | flops 2359296 | bytes 9437184 | tf_op jit(solution)/shard_map/stack | solution.py:42
  68.1 8.5 %copy.112 = bf16[2,2,384,4,384]{2,3,4,1,0:T(4,128)(2,1)} copy(bf16[2,2,384,4,384]{4,2,3,1,0:T(8,128)(2,1)} %pad_maximum_fusion) | data formatting | bytes 9437184 | tf_op jit(solution)/shard_map/stack | solution.py:42
  76.6 20.7 %gather_fusion = bf16[384,2,2,384,4]{3,4,2,1,0:T(4,128)(2,1)} fusion(bf16[2,2,384,4,384]{2,3,4,1,0:T(4,128)(2,1)} %copy.112, s32[1024]{0:T(1024)S(1)} %pad_clamp_fusion), kind=kCustom, calls=%fused_computation.4 | custom fusion | bytes 9438720 | tf_op jit(solution)/shard_map/jit(_take)/gather | solution.py:43
  97.3 6.8 %select_bitcast_fusion = bf16[2,2,384,4,384]{2,3,1,0,4:T(4,128)(2,1)} fusion(bf16[384,2,2,384,4]{3,4,2,1,0:T(4,128)(2,1)} %gather_fusion, pred[384]{0:T(512)(128)(4,1)S(1)} %compare_and_fusion.2), kind=kLoop, calls=%fused_computation.14 | loop fusion | flops 2359296 | bytes 9437568 | tf_op jit(solution)/shard_map/jit(_take)/select_n | solution.py:43
  104.1 10.3 %copy.113 = bf16[2,2,384,4,384]{4,3,1,0,2:T(4,128)(2,1)} copy(bf16[2,2,384,4,384]{2,3,1,0,4:T(4,128)(2,1)} %select_bitcast_fusion) | data formatting | bytes 9437184 | tf_op jit(solution)/shard_map/jit(_take)/select_n | solution.py:43
  114.4 110.1 %all_to_all.18 = bf16[2,2,384,4,384]{4,3,1,0,2:T(4,128)(2,1)S(1)} all-to-all(bf16[2,2,384,4,384]{4,3,1,0,2:T(4,128)(2,1)} %copy.113), channel_id=1, replica_groups=mesh['freq'=4,'bond'=8] {'bond'}, dimensions={2} | all-to-all | bytes 9437184 | tf_op jit(solution)/shard_map/all_to_all | solution.py:73
  224.5 1.1 copy.114
  225.6 0.8 copy.115
  226.4 3.2 %copy.116 = bf16[2,2,48,32,384]{4,3,2,1,0:T(8,128)(2,1)} copy(bf16[2,2,48,32,384]{4,2,3,1,0:T(8,128)(2,1)S(1)} %bitcast.112) | data formatting | bytes 9437184 | tf_op jit(solution)/shard_map/all_to_all | solution.py:73
  (38 shorter events, 7.0 us)
Async XLA Ops:
  41.5 7.1 %slice-start = ((s8[4718592]{0:T(1024)(128)(4,1)}), s8[4194304]{0:T(1024)(128)(4,1)S(1)}, s32[]{:S(2)}) async-start(s8[4718592]{0:T(1024)(128)(4,1)} %bitcast.114), calls=%async_computation.1 | async-start | bytes 8388608
  41.7 7.0 %slice-start.1 = ((s8[4718592]{0:T(1024)(128)(4,1)}), s8[524288]{0:T(1024)(128)(4,1)S(1)}, s32[]{:S(2)}) async-start(s8[4718592]{0:T(1024)(128)(4,1)} %bitcast.114), calls=%async_computation.2 | async-start | bytes 1048576
  48.7 3.8 %copy-start = (s32[384]{0:T(512)S(1)}, s32[384]{0:T(512)}, u32[]{:S(2)}) copy-start(s32[384]{0:T(512)} %param.15) | copy-start | bytes 4612
  48.7 3.8 %copy-start.1 = (s32[2,3,3]{2,0,1:T(2,128)S(1)}, s32[2,3,3]{2,0,1:T(2,128)}, u32[]{:S(2)}) copy-start(s32[2,3,3]{2,0,1:T(2,128)} %param.14) | copy-start | bytes 220
where the time goes:
time: 231 us; the launch traced here: 230 us
  blocking collectives  128 us (55%)
  local copies, waits for them, and re-layouts  64.3 us (28%)
  matrix products  23 us (10%)
  other arithmetic  14.1 us (6%)
    all_to_all x1, blocking collectives, body(): lax.all_to_all(flows, 'bond', split_axis=2, concat_axis=3, tiled=True)  110 us
    dot_general x4, matrix products, products(): return jnp.einsum(pattern, left, right, preferred_element_type=jnp.float32)  23 us
    gather x1, local copies, waits for them, and re-layouts, compute_flows(): return jnp.take(rounded, site_perm, axis=4)  20.7 us
    select_n x1, local copies, waits for them, and re-layouts, compute_flows(): return jnp.take(rounded, site_perm, axis=4)  10.3 us
    all_gather x1, blocking collectives, body(): lax.all_gather(green, 'freq', axis=1, tiled=True)  9.71 us
    another operation x1, local copies, waits for them, and re-layouts, compute_flows(): rounded = jnp.stack([flow_real, flow_imag]).astype(jnp.bfloat16)  8.47 us
    all_gather x1, blocking collectives, body(): lax.all_gather(single, 'freq', axis=1, tiled=True)  8.2 us
    select_n x2, other arithmetic, compute_flows(): return jnp.take(rounded, site_perm, axis=4)  6.84 us

commit v1 on v0

v1 whole, which is shorter than its diff:
```python
import functools
import math

import jax
import jax.numpy as jnp
from jax import lax
from jax.experimental import pallas as pl
from jax.experimental.pallas import tpu as pltpu
from jax.sharding import PartitionSpec as P

LANES = 128


def partner(index, step, count):
    if count & (count - 1):
        return lax.rem(index + step, count)
    found = 0
    bit = 1
    while bit < count:
        found = found + lax.rem(index // bit + (step // bit) % 2, 2) * bit
        bit *= 2
    return found


def origin(index, step, count):
    if count & (count - 1):
        return lax.rem(index + count - step, count)
    return partner(index, step, count)


def times_complex(a, b, c, d):
    return a * c - b * d, a * d + b * c


def kernel(nf, nb, gamma, green, single, bond, mask, perm, out,
           all_green, all_single, bubble, masks, shuffle, send, land, stage,
           recv_g, recv_s, send_g, send_s, send_sem, recv_sem, own_sem):
    _, local, sites_here, order, _ = gamma.shape
    sites = green.shape[-1]
    blocks = mask.shape[-1]
    width = order // blocks
    rows = order // nb
    count = local * nf
    seg = nb * sites_here
    items = local * sites_here
    f = lax.axis_index("freq")
    b = lax.axis_index("bond")

    barrier = pltpu.get_barrier_semaphore()
    for step in range(1, nf):
        pl.semaphore_signal(barrier, inc=1, device_id={"freq": lax.rem(f + step, nf)},
                            device_id_type=pl.DeviceIdType.MESH)
    for step in range(1, nb):
        pl.semaphore_signal(barrier, inc=1, device_id={"bond": partner(b, step, nb)},
                            device_id_type=pl.DeviceIdType.MESH)
    pl.semaphore_wait(barrier, nf - 1 + nb - 1)

    def greens(step):
        to = lax.rem(f + step, nf)
        pair = []
        for source, landing, ss, rs in ((green, all_green, send_g, recv_g),
                                        (single, all_single, send_s, recv_s)):
            pair.append(pltpu.make_async_remote_copy(
                src_ref=source, dst_ref=landing.at[f], send_sem=ss.at[step],
                recv_sem=rs.at[step], device_id={"freq": to},
                device_id_type=pl.DeviceIdType.MESH))
        return pair

    for step in range(1, nf):
        for copy in greens(step):
            copy.start()
    all_green[f] = green[...]
    all_single[f] = single[...]

    pick = (lax.broadcasted_iota(jnp.int32, (sites, order), 0) == bond[...]).astype(jnp.float32)
    shuffle[...] = (lax.broadcasted_iota(jnp.int32, (order, order), 0) == perm[...]).astype(
        jnp.float32).astype(jnp.bfloat16)
    for w in range(local):
        for i in range(blocks):
            for j in range(blocks):
                masks[w, i * width:(i + 1) * width, j * width:(j + 1) * width] = jnp.full(
                    (width, width), mask[w, i, j].astype(jnp.float32), jnp.float32)

    for step in range(1, nf):
        for copy in greens(step):
            copy.wait()

    factor = 1.0 / math.sqrt(count)
    for w in range(local):
        real = jnp.zeros((sites_here, sites), jnp.float32)
        imag = jnp.zeros((sites_here, sites), jnp.float32)
        for v in range(count):
            moved = lax.rem(f * local + (w + v), count)
            far, near = moved // local, lax.rem(moved, local)
            g = [all_green[v // local, part, v % local] for part in range(2)]
            s = [all_single[v // local, part, v % local] for part in range(2)]
            gm = [all_green[far, part, near] for part in range(2)]
            sm = [all_single[far, part, near] for part in range(2)]
            first = times_complex(g[0], g[1], sm[0], sm[1])
            second = times_complex(s[0], s[1], gm[0], gm[1])
            real = real + (first[0] + second[0])
            imag = imag + (first[1] + second[1])
        for part, value in enumerate((real, imag)):
            bubble[part, w] = jnp.dot(value * factor, pick, precision=lax.Precision.HIGHEST,
                                      preferred_element_type=jnp.float32)

    def own(i):
        return pltpu.make_async_copy(send.at[i, b], land.at[i, b], own_sem.at[i])

    def outgoing(i, step):
        to = partner(b, step, nb)
        return pltpu.make_async_remote_copy(
            src_ref=send.at[i, to], dst_ref=land.at[i, b], send_sem=send_sem.at[i, step],
            recv_sem=recv_sem.at[i, step], device_id={"bond": to},
            device_id_type=pl.DeviceIdType.MESH)

    def compute(i, carry):
        w, s = i // sites_here, lax.rem(i, sites_here)
        gr, gi = gamma[0, w, s], gamma[1, w, s]
        br, bi = bubble[0, w, pl.ds(s, 1), :], bubble[1, w, pl.ds(s, 1), :]
        grf, gif = gr.astype(jnp.float32), gi.astype(jnp.float32)
        lr = (grf * br - gif * bi).astype(jnp.bfloat16)
        li = (grf * bi + gif * br).astype(jnp.bfloat16)
        left = jnp.concatenate([lr, li], axis=1)
        fr = jnp.dot(left, jnp.concatenate([gr, -gi], axis=0), preferred_element_type=jnp.float32)
        fi = jnp.dot(left, jnp.concatenate([gi, gr], axis=0), preferred_element_type=jnp.float32)
        for part, flow in enumerate((fr, fi)):
            kept = (flow * masks[w]).astype(jnp.bfloat16)
            moved = jnp.dot(kept, shuffle[...], preferred_element_type=jnp.float32).astype(jnp.bfloat16)
            for d in range(nb):
                send[i, d, part] = moved[d * rows:(d + 1) * rows]
        for step in range(nb - 1, 0, -1):
            outgoing(i, step).start()
        own(i).start()
        return carry

    lax.fori_loop(0, items, compute, 0)

    def arrange(i, src):
        w, s = i // sites_here, lax.rem(i, sites_here)
        for part in range(2):
            block = land[i, src, part].astype(jnp.float32)
            for c in range(order // LANES):
                stage[w, part, c, pl.ds(src * sites_here + s, rows, stride=seg), :] = (
                    block[:, c * LANES:(c + 1) * LANES])

    def receive(i, carry):
        own(i).wait()
        arrange(i, b)
        for step in range(1, nb):
            copy = outgoing(i, step)
            copy.wait_recv()
            arrange(i, origin(b, step, nb))
        return carry

    for w in range(local):
        lax.fori_loop(w * sites_here, (w + 1) * sites_here, receive, 0)
        for part in range(2):
            for c in range(order // LANES):
                out[part, w, :, :, c * LANES:(c + 1) * LANES] = (
                    stage[w, part, c].reshape(rows, seg, LANES).astype(jnp.bfloat16))

    def drain(i, carry):
        for step in range(1, nb):
            outgoing(i, step).wait_send()
        return carry

    lax.fori_loop(0, items, drain, 0)


def body(nf, nb, gamma, green, single, bond_site, causal_mask, site_perm):
    _, local, sites_here, order, _ = gamma.shape
    sites = green.shape[-1]
    rows = order // nb
    seg = nb * sites_here
    items = local * sites_here
    vmem = pl.BlockSpec(memory_space=pltpu.VMEM)
    dma = pltpu.SemaphoreType.DMA
    return pl.pallas_call(
        functools.partial(kernel, nf, nb),
        out_shape=jax.ShapeDtypeStruct((2, local, rows, seg, order), jnp.bfloat16),
        in_specs=[vmem, vmem, vmem, vmem, pl.BlockSpec(memory_space=pltpu.SMEM), vmem],
        out_specs=vmem,
        scratch_shapes=[
            pltpu.VMEM((nf, 2, local, sites_here, sites), jnp.float32),
            pltpu.VMEM((nf, 2, local, sites_here, sites), jnp.float32),
            pltpu.VMEM((2, local, sites_here, order), jnp.float32),
            pltpu.VMEM((local, order, order), jnp.float32),
            pltpu.VMEM((order, order), jnp.bfloat16),
            pltpu.VMEM((items, nb, 2, rows, order), jnp.bfloat16),
            pltpu.VMEM((items, nb, 2, rows, order), jnp.bfloat16),
            pltpu.VMEM((local, 2, order // LANES, rows * seg, LANES), jnp.float32),
            dma((nf,)), dma((nf,)), dma((nf,)), dma((nf,)),
            dma((items, nb)), dma((items, nb)), dma((items,)),
        ],
        compiler_params=pltpu.CompilerParams(
            collective_id=0, has_side_effects=True, vmem_limit_bytes=60 * 1024 * 1024),
        name="flow_exchange",
    )(gamma, green, single, bond_site[None, :], causal_mask, site_perm[None, :])


def solution(mesh):
    in_specs = (
        P(None, "freq", "bond", None, None),
        P(None, "freq", "bond", None),
        P(None, "freq", "bond", None),
        P(),
        P("freq", None, None),
        P(),
    )
    out_specs = P(None, "freq", "bond", None, None)
    run = functools.partial(body, mesh.shape["freq"], mesh.shape["bond"])
    return jax.shard_map(run, mesh=mesh, in_specs=in_specs, out_specs=out_specs, check_vma=False)
```

time: 231 us -> 129 us (0.56)
  blocking collectives: 128 us -> 0 us
  Pallas kernels: 0 us -> 120 us
  local copies, waits for them, and re-layouts: 64.3 us -> 8.85 us
  matrix products: 23 us -> 0 us
  other arithmetic: 14.1 us -> 0 us
    pallas_call x0 -> x1, Pallas kernels: none -> 120 us  [body(): pl.pallas_call(functools.partial(kernel, nf, nb), out_shape=jax.ShapeDtyp...]
    all_to_all x1 -> x0, blocking collectives: 110 us -> none  [body(): lax.all_to_all(flows, 'bond', split_axis=2, concat_axis=3, tiled=True)]
    gather x5 -> x0, local copies, waits for them, and re-layouts: 28.3 us -> none  [the longest x1 20.7 us: compute_flows(): return jnp.take(rounded, site_perm, axis=4)]
    dot_general x4 -> x0, matrix products: 23 us -> none  [products(): return jnp.einsum(pattern, left, right, preferred_element_type=jnp.float32)]
    all_gather x2 -> x0, blocking collectives: 17.9 us -> none  [the longest x1 9.71 us: body(): lax.all_gather(green, 'freq', axis=1, tiled=True)]
    select_n x3 -> x0, local copies, waits for them, and re-layouts: 12 us -> none  [the longest x1 10.3 us: compute_flows(): return jnp.take(rounded, site_perm, axis=4)]
    select_n x6 -> x0, other arithmetic: 10.5 us -> none  [the longest x2 6.84 us: compute_flows(): return jnp.take(rounded, site_perm, axis=4)]
    another operation x1 -> x0, local copies, waits for them, and re-layouts: 8.47 us -> none  [compute_flows(): rounded = jnp.stack([flow_real, flow_imag]).astype(jnp.bfloat16)]
where the time goes in v1:
time: 129 us
  Pallas kernels  120 us (93%)
  local copies, waits for them, and re-layouts  8.85 us (7%)
    pallas_call x1, Pallas kernels, body(): pl.pallas_call(functools.partial(kernel, nf, nb), out_shape=jax.ShapeDtyp...  120 us
    unnamed x2, local copies, waits for them, and re-layouts  6.35 us

profile of v1, /device:TPU:0, one launch (start us, length us, event | category | flops | bytes accessed | tf_op | source)
XLA Modules:
  0.0 128.9 jit_solution(2678350849044603500)
XLA Ops:
  0.0 1.2 broadcast_in_dim.6.bond
  1.2 1.3 broadcast_in_dim.7.perm
  2.5 1.3 copy.7.mask
  3.8 120.0 %flow_exchange.1 = bf16[2,2,48,32,384]{4,3,2,1,0:T(8,128)(2,1)} custom-call(bf16[2,2,4,384,384]{4,3,2,1,0:T(8,128)(2,1)} %gamma.1, f32[2,2,4,256]{3,2,1,0:T(4,128)} %green.1, f32[2,2,4,256]{3,2,1,0:T(4,128)} %single.1, s32[1,384]{1,0:T(1,128)} %broadcast_in_dim.6.bond, s32[2,3,3]{2,1,0:T(4,128)} %copy.7.mask, s32[1,384]{1,0:T(1,128)} %broadcast_in_dim.7.perm), custom_call_target="tpu_custom_call" | custom-call | tf_op jit(solution)/shard_map/flow_exchange/pallas_call | solution.py:179
  123.8 5.1 %copy.9 = bf16[2,2,48,32,384]{4,3,2,1,0:T(8,128)(2,1)} copy(bf16[2,2,48,32,384]{4,3,2,1,0:T(8,128)(2,1)} %flow_exchange.1) | data formatting | bytes 9437184

commit v2 on v1

--- a/solution.py
+++ b/solution.py
@@ -9,6 +9,7 @@
 from jax.sharding import PartitionSpec as P
 
 LANES = 128
+WINDOW = 2
 
 
 def partner(index, step, count):
@@ -72,14 +73,14 @@
     all_green[f] = green[...]
     all_single[f] = single[...]
 
-    pick = (lax.broadcasted_iota(jnp.int32, (sites, order), 0) == bond[...]).astype(jnp.float32)
-    shuffle[...] = (lax.broadcasted_iota(jnp.int32, (order, order), 0) == perm[...]).astype(
+    pick = (lax.broadcasted_iota(jnp.int32, (sites, order), 0) == bond[...][None, :]).astype(jnp.float32)
+    shuffle[...] = (lax.broadcasted_iota(jnp.int32, (order, order), 0) == perm[...][None, :]).astype(
         jnp.float32).astype(jnp.bfloat16)
     for w in range(local):
         for i in range(blocks):
             for j in range(blocks):
                 masks[w, i * width:(i + 1) * width, j * width:(j + 1) * width] = jnp.full(
-                    (width, width), mask[w, i, j].astype(jnp.float32), jnp.float32)
+                    (width, width), mask[i, w, j].astype(jnp.float32), jnp.float32)
 
     for step in range(1, nf):
         for copy in greens(step):
@@ -129,12 +130,15 @@
             moved = jnp.dot(kept, shuffle[...], preferred_element_type=jnp.float32).astype(jnp.bfloat16)
             for d in range(nb):
                 send[i, d, part] = moved[d * rows:(d + 1) * rows]
+
+        @pl.when(i >= WINDOW)
+        def _():
+            receive(i - WINDOW)
+
         for step in range(nb - 1, 0, -1):
             outgoing(i, step).start()
         own(i).start()
         return carry
-
-    lax.fori_loop(0, items, compute, 0)
 
     def arrange(i, src):
         w, s = i // sites_here, lax.rem(i, sites_here)
@@ -144,17 +148,21 @@
                 stage[w, part, c, pl.ds(src * sites_here + s, rows, stride=seg), :] = (
                     block[:, c * LANES:(c + 1) * LANES])
 
-    def receive(i, carry):
+    def receive(i):
         own(i).wait()
         arrange(i, b)
         for step in range(1, nb):
             copy = outgoing(i, step)
             copy.wait_recv()
             arrange(i, origin(b, step, nb))
+
+    def receive_last(i, carry):
+        receive(i)
         return carry
 
+    lax.fori_loop(0, items, compute, 0)
+    lax.fori_loop(items - WINDOW, items, receive_last, 0)
     for w in range(local):
-        lax.fori_loop(w * sites_here, (w + 1) * sites_here, receive, 0)
         for part in range(2):
             for c in range(order // LANES):
                 out[part, w, :, :, c * LANES:(c + 1) * LANES] = (
@@ -196,7 +204,7 @@
         compiler_params=pltpu.CompilerParams(
             collective_id=0, has_side_effects=True, vmem_limit_bytes=60 * 1024 * 1024),
         name="flow_exchange",
-    )(gamma, green, single, bond_site[None, :], causal_mask, site_perm[None, :])
+    )(gamma, green, single, bond_site, causal_mask.transpose(1, 0, 2), site_perm)
 
 
 def solution(mesh):

time: 129 us -> 126 us (0.977)
  local copies, waits for them, and re-layouts: 8.85 us -> 5.07 us
    broadcast_in_dim x2 -> x0, local copies, waits for them, and re-layouts: 2.5 us -> none  [the longest x1 1.26 us: body(): site_perm[None, :]]
    unnamed x2 -> x1, local copies, waits for them, and re-layouts: 6.35 us -> 5.07 us
where the time goes in v2:
time: 126 us
  Pallas kernels  121 us (96%)
  local copies, waits for them, and re-layouts  5.07 us (4%)
    pallas_call x1, Pallas kernels, body(): pl.pallas_call(functools.partial(kernel, nf, nb), out_shape=jax.ShapeDtyp...  121 us
    unnamed x1, local copies, waits for them, and re-layouts  5.07 us

profile of v2, /device:TPU:0, one launch (start us, length us, event | category | flops | bytes accessed | tf_op | source)
XLA Modules:
  0.0 125.7 jit_solution(10340191931211679024)
XLA Ops:
  0.0 120.6 %flow_exchange.1 = bf16[2,2,48,32,384]{4,3,2,1,0:T(8,128)(2,1)} custom-call(bf16[2,2,4,384,384]{4,3,2,1,0:T(8,128)(2,1)} %gamma.1, f32[2,2,4,256]{3,2,1,0:T(4,128)} %green.1, f32[2,2,4,256]{3,2,1,0:T(4,128)} %single.1, s32[384]{0:T(512)} %bond.1, s32[3,2,3]{2,1,0:T(2,128)} %bitcast.1, s32[384]{0:T(512)} %perm.1), custom_call_target="tpu_custom_call" | custom-call | tf_op jit(solution)/shard_map/flow_exchange/pallas_call | solution.py:187
  120.6 5.1 %copy.8 = bf16[2,2,48,32,384]{4,3,2,1,0:T(8,128)(2,1)} copy(bf16[2,2,48,32,384]{4,3,2,1,0:T(8,128)(2,1)} %flow_exchange.1) | data formatting | bytes 9437184

commit v3 on v2

--- a/solution.py
+++ b/solution.py
@@ -10,6 +10,7 @@
 
 LANES = 128
 WINDOW = 2
+VMEM_BYTES = 67_043_328
 
 
 def partner(index, step, count):
@@ -33,10 +34,10 @@
     return a * c - b * d, a * d + b * c
 
 
-def kernel(nf, nb, gamma, green, single, bond, mask, perm, out,
-           all_green, all_single, bubble, masks, shuffle, send, land, stage,
+def kernel(nf, nb, gamma_hbm, green, single, bond, mask, perm, out,
+           gamma, gamma_sem, all_green, all_single, bubble, masks, shuffle, send, land, stage,
            recv_g, recv_s, send_g, send_s, send_sem, recv_sem, own_sem):
-    _, local, sites_here, order, _ = gamma.shape
+    _, local, sites_here, order, _ = gamma_hbm.shape
     sites = green.shape[-1]
     blocks = mask.shape[-1]
     width = order // blocks
@@ -47,6 +48,14 @@
     f = lax.axis_index("freq")
     b = lax.axis_index("bond")
 
+    def fetch(i):
+        w, s = i // sites_here, lax.rem(i, sites_here)
+        return pltpu.make_async_copy(gamma_hbm.at[:, w, s], gamma.at[i], gamma_sem.at[i])
+
+    def fetch_start(i, carry):
+        fetch(i).start()
+        return carry
+
     barrier = pltpu.get_barrier_semaphore()
     for step in range(1, nf):
         pl.semaphore_signal(barrier, inc=1, device_id={"freq": lax.rem(f + step, nf)},
@@ -54,6 +63,17 @@
     for step in range(1, nb):
         pl.semaphore_signal(barrier, inc=1, device_id={"bond": partner(b, step, nb)},
                             device_id_type=pl.DeviceIdType.MESH)
+    lax.fori_loop(0, items, fetch_start, 0)
+
+    pick = (lax.broadcasted_iota(jnp.int32, (sites, order), 0) == bond[...][None, :]).astype(jnp.float32)
+    shuffle[...] = (lax.broadcasted_iota(jnp.int32, (order, order), 0) == perm[...][None, :]).astype(
+        jnp.float32).astype(jnp.bfloat16)
+    for w in range(local):
+        for i in range(blocks):
+            for j in range(blocks):
+                masks[w, i * width:(i + 1) * width, j * width:(j + 1) * width] = jnp.full(
+                    (width, width), mask[i, w, j].astype(jnp.float32), jnp.float32)
+
     pl.semaphore_wait(barrier, nf - 1 + nb - 1)
 
     def greens(step):
@@ -72,15 +92,6 @@
             copy.start()
     all_green[f] = green[...]
     all_single[f] = single[...]
-
-    pick = (lax.broadcasted_iota(jnp.int32, (sites, order), 0) == bond[...][None, :]).astype(jnp.float32)
-    shuffle[...] = (lax.broadcasted_iota(jnp.int32, (order, order), 0) == perm[...][None, :]).astype(
-        jnp.float32).astype(jnp.bfloat16)
-    for w in range(local):
-        for i in range(blocks):
-            for j in range(blocks):
-                masks[w, i * width:(i + 1) * width, j * width:(j + 1) * width] = jnp.full(
-                    (width, width), mask[i, w, j].astype(jnp.float32), jnp.float32)
 
     for step in range(1, nf):
         for copy in greens(step):
@@ -115,27 +126,37 @@
             recv_sem=recv_sem.at[i, step], device_id={"bond": to},
             device_id_type=pl.DeviceIdType.MESH)
 
+    half_rows, half_count = order // 2, nb // 2
+
     def compute(i, carry):
         w, s = i // sites_here, lax.rem(i, sites_here)
-        gr, gi = gamma[0, w, s], gamma[1, w, s]
+        fetch(i).wait()
+        gr, gi = gamma[i, 0], gamma[i, 1]
         br, bi = bubble[0, w, pl.ds(s, 1), :], bubble[1, w, pl.ds(s, 1), :]
-        grf, gif = gr.astype(jnp.float32), gi.astype(jnp.float32)
-        lr = (grf * br - gif * bi).astype(jnp.bfloat16)
-        li = (grf * bi + gif * br).astype(jnp.bfloat16)
-        left = jnp.concatenate([lr, li], axis=1)
-        fr = jnp.dot(left, jnp.concatenate([gr, -gi], axis=0), preferred_element_type=jnp.float32)
-        fi = jnp.dot(left, jnp.concatenate([gi, gr], axis=0), preferred_element_type=jnp.float32)
-        for part, flow in enumerate((fr, fi)):
-            kept = (flow * masks[w]).astype(jnp.bfloat16)
-            moved = jnp.dot(kept, shuffle[...], preferred_element_type=jnp.float32).astype(jnp.bfloat16)
-            for d in range(nb):
-                send[i, d, part] = moved[d * rows:(d + 1) * rows]
-
-        @pl.when(i >= WINDOW)
-        def _():
-            receive(i - WINDOW)
-
-        for step in range(nb - 1, 0, -1):
+        right_real = jnp.concatenate([gr, -gi], axis=0)
+        right_imag = jnp.concatenate([gi, gr], axis=0)
+        own_half = b // half_count
+        for turn in range(2):
+            half = lax.rem(own_half + 1 + turn, 2)
+            top = pl.ds(pl.multiple_of(half * half_rows, half_rows), half_rows)
+            grf, gif = gamma[i, 0, top, :].astype(jnp.float32), gamma[i, 1, top, :].astype(jnp.float32)
+            lr = (grf * br - gif * bi).astype(jnp.bfloat16)
+            li = (grf * bi + gif * br).astype(jnp.bfloat16)
+            left = jnp.concatenate([lr, li], axis=1)
+            for part, right in enumerate((right_real, right_imag)):
+                flow = jnp.dot(left, right, preferred_element_type=jnp.float32)
+                kept = (flow * masks[w, top, :]).astype(jnp.bfloat16)
+                moved = jnp.dot(kept, shuffle[...], preferred_element_type=jnp.float32).astype(jnp.bfloat16)
+                for d in range(half_count):
+                    send[i, half * half_count + d, part] = moved[d * rows:(d + 1) * rows]
+            if turn == 0:
+                @pl.when(i >= WINDOW)
+                def _():
+                    receive(i - WINDOW)
+
+                for step in range(nb - 1, half_count - 1, -1):
+                    outgoing(i, step).start()
+        for step in range(half_count - 1, 0, -1):
             outgoing(i, step).start()
         own(i).start()
         return carry
@@ -156,18 +177,20 @@
             copy.wait_recv()
             arrange(i, origin(b, step, nb))
 
+        @pl.when(lax.rem(i, sites_here) == sites_here - 1)
+        def _():
+            w = i // sites_here
+            for part in range(2):
+                for c in range(order // LANES):
+                    out[part, w, :, :, c * LANES:(c + 1) * LANES] = (
+                        stage[w, part, c].reshape(rows, seg, LANES).astype(jnp.bfloat16))
+
     def receive_last(i, carry):
         receive(i)
         return carry
 
     lax.fori_loop(0, items, compute, 0)
     lax.fori_loop(items - WINDOW, items, receive_last, 0)
-    for w in range(local):
-        for part in range(2):
-            for c in range(order // LANES):
-                out[part, w, :, :, c * LANES:(c + 1) * LANES] = (
-                    stage[w, part, c].reshape(rows, seg, LANES).astype(jnp.bfloat16))
-
     def drain(i, carry):
         for step in range(1, nb):
             outgoing(i, step).wait_send()
@@ -182,14 +205,17 @@
     rows = order // nb
     seg = nb * sites_here
     items = local * sites_here
+    result_bytes = 2 * local * rows * seg * order * 2
     vmem = pl.BlockSpec(memory_space=pltpu.VMEM)
     dma = pltpu.SemaphoreType.DMA
     return pl.pallas_call(
         functools.partial(kernel, nf, nb),
-        out_shape=jax.ShapeDtypeStruct((2, local, rows, seg, order), jnp.bfloat16),
-        in_specs=[vmem, vmem, vmem, vmem, pl.BlockSpec(memory_space=pltpu.SMEM), vmem],
+        out_shape=pltpu.VMEM((2, local, rows, seg, order), jnp.bfloat16),
+        in_specs=[pl.BlockSpec(memory_space=pl.ANY), vmem, vmem, vmem, pl.BlockSpec(memory_space=pltpu.SMEM), vmem],
         out_specs=vmem,
         scratch_shapes=[
+            pltpu.VMEM((items, 2, order, order), jnp.bfloat16),
+            dma((items,)),
             pltpu.VMEM((nf, 2, local, sites_here, sites), jnp.float32),
             pltpu.VMEM((nf, 2, local, sites_here, sites), jnp.float32),
             pltpu.VMEM((2, local, sites_here, order), jnp.float32),
@@ -202,7 +228,7 @@
             dma((items, nb)), dma((items, nb)), dma((items,)),
         ],
         compiler_params=pltpu.CompilerParams(
-            collective_id=0, has_side_effects=True, vmem_limit_bytes=60 * 1024 * 1024),
+            collective_id=0, has_side_effects=True, vmem_limit_bytes=VMEM_BYTES - result_bytes),
         name="flow_exchange",
     )(gamma, green, single, bond_site, causal_mask.transpose(1, 0, 2), site_perm)
 

time: 126 us -> 119 us (0.944)
  Pallas kernels: 121 us -> 116 us
  local copies, waits for them, and re-layouts: 5.07 us -> 2.19 us
    pallas_call x1, Pallas kernels: 121 us -> 116 us  [body(): pl.pallas_call(functools.partial(kernel, nf, nb), out_shape=pltpu.VMEM((2...]
    unnamed x1, local copies, waits for them, and re-layouts: 5.07 us -> 2.19 us
where the time goes in v3:
time: 119 us
  Pallas kernels  116 us (97%)
  local copies, waits for them, and re-layouts  2.19 us (2%)
    pallas_call x1, Pallas kernels, body(): pl.pallas_call(functools.partial(kernel, nf, nb), out_shape=pltpu.VMEM((2...  116 us

profile of v3, /device:TPU:0, one launch (start us, length us, event | category | flops | bytes accessed | tf_op | source)
XLA Modules:
  0.0 118.6 jit_solution(14643929020890343330)
XLA Ops:
  0.0 116.4 %flow_exchange.1 = bf16[2,2,48,32,384]{4,3,2,1,0:T(8,128)(2,1)S(1)} custom-call(bf16[2,2,4,384,384]{4,3,2,1,0:T(8,128)(2,1)} %gamma_hbm.1, f32[2,2,4,256]{3,2,1,0:T(4,128)} %green.1, f32[2,2,4,256]{3,2,1,0:T(4,128)} %single.1, s32[384]{0:T(512)} %bond.1, s32[3,2,3]{2,1,0:T(2,128)} %bitcast.1, s32[384]{0:T(512)} %perm.1), custom_call_target="tpu_custom_call" | custom-call | tf_op jit(solution)/shard_map/flow_exchange/pallas_call | solution.py:211
  116.4 2.2 %copy.8 = bf16[2,2,48,32,384]{4,3,2,1,0:T(8,128)(2,1)} copy(bf16[2,2,48,32,384]{4,3,2,1,0:T(8,128)(2,1)S(1)} %flow_exchange.1) | data formatting | bytes 9437184

commit v4 on v3

--- a/solution.py
+++ b/solution.py
@@ -127,6 +127,10 @@
             device_id_type=pl.DeviceIdType.MESH)
 
     half_rows, half_count = order // 2, nb // 2
+
+    def send_steps(i, high, low):
+        for step in range(high, low, -1):
+            outgoing(i, step).start()
 
     def compute(i, carry):
         w, s = i // sites_here, lax.rem(i, sites_here)
@@ -150,14 +154,20 @@
                 for d in range(half_count):
                     send[i, half * half_count + d, part] = moved[d * rows:(d + 1) * rows]
             if turn == 0:
-                @pl.when(i >= WINDOW)
+                @pl.when(i == 0)
                 def _():
-                    receive(i - WINDOW)
-
-                for step in range(nb - 1, half_count - 1, -1):
-                    outgoing(i, step).start()
-        for step in range(half_count - 1, 0, -1):
-            outgoing(i, step).start()
+                    send_steps(i, nb - 1, half_count - 1)
+
+        @pl.when(i >= WINDOW)
+        def _():
+            receive(i - WINDOW)
+
+        send_steps(i, half_count - 1, 0)
+
+        @pl.when(i > 0)
+        def _():
+            send_steps(i, nb - 1, half_count - 1)
+
         own(i).start()
         return carry
 

time: 119 us -> 119 us (level)
  no operation moved by 1% of the time
where the time goes in v4:
time: 119 us
  Pallas kernels  116 us (97%)
  local copies, waits for them, and re-layouts  2.19 us (2%)
    pallas_call x1, Pallas kernels, body(): pl.pallas_call(functools.partial(kernel, nf, nb), out_shape=pltpu.VMEM((2...  116 us

profile of v4, /device:TPU:0, one launch (start us, length us, event | category | flops | bytes accessed | tf_op | source)
XLA Modules:
  0.0 118.5 jit_solution(12589636723334166842)
XLA Ops:
  0.0 116.3 %flow_exchange.1 = bf16[2,2,48,32,384]{4,3,2,1,0:T(8,128)(2,1)S(1)} custom-call(bf16[2,2,4,384,384]{4,3,2,1,0:T(8,128)(2,1)} %gamma_hbm.1, f32[2,2,4,256]{3,2,1,0:T(4,128)} %green.1, f32[2,2,4,256]{3,2,1,0:T(4,128)} %single.1, s32[384]{0:T(512)} %bond.1, s32[3,2,3]{2,1,0:T(2,128)} %bitcast.1, s32[384]{0:T(512)} %perm.1), custom_call_target="tpu_custom_call" | custom-call | tf_op jit(solution)/shard_map/flow_exchange/pallas_call | solution.py:221
  116.3 2.2 %copy.8 = bf16[2,2,48,32,384]{4,3,2,1,0:T(8,128)(2,1)} copy(bf16[2,2,48,32,384]{4,3,2,1,0:T(8,128)(2,1)S(1)} %flow_exchange.1) | data formatting | bytes 9437184

commit v5 on v4

--- a/solution.py
+++ b/solution.py
@@ -34,12 +34,12 @@
     return a * c - b * d, a * d + b * c
 
 
-def kernel(nf, nb, gamma_hbm, green, single, bond, mask, perm, out,
-           gamma, gamma_sem, all_green, all_single, bubble, masks, shuffle, send, land, stage,
+def kernel(nf, nb, gamma_hbm, green, single, bond_hbm, mask_hbm, perm_hbm, out,
+           gamma, gamma_sem, bond, mask, perm, values, small_sem, all_green, all_single, bubble, masks, shuffle, send, land, stage,
            recv_g, recv_s, send_g, send_s, send_sem, recv_sem, own_sem):
     _, local, sites_here, order, _ = gamma_hbm.shape
     sites = green.shape[-1]
-    blocks = mask.shape[-1]
+    blocks = mask_hbm.shape[-1]
     width = order // blocks
     rows = order // nb
     count = local * nf
@@ -63,9 +63,20 @@
     for step in range(1, nb):
         pl.semaphore_signal(barrier, inc=1, device_id={"bond": partner(b, step, nb)},
                             device_id_type=pl.DeviceIdType.MESH)
+    small = [
+        pltpu.make_async_copy(source, kept, small_sem.at[k])
+        for k, (source, kept) in enumerate((
+            (bond_hbm, bond), (perm_hbm, perm), (mask_hbm, mask),
+            (green, all_green.at[f]), (single, all_single.at[f])))
+    ]
+    for copy in small:
+        copy.start()
     lax.fori_loop(0, items, fetch_start, 0)
-
-    pick = (lax.broadcasted_iota(jnp.int32, (sites, order), 0) == bond[...][None, :]).astype(jnp.float32)
+    for copy in small:
+        copy.wait()
+
+    pick = (lax.broadcasted_iota(jnp.int32, (sites, order), 0) == bond[...][None, :]).astype(
+        jnp.float32).astype(jnp.bfloat16)
     shuffle[...] = (lax.broadcasted_iota(jnp.int32, (order, order), 0) == perm[...][None, :]).astype(
         jnp.float32).astype(jnp.bfloat16)
     for w in range(local):
@@ -90,8 +101,6 @@
     for step in range(1, nf):
         for copy in greens(step):
             copy.start()
-    all_green[f] = green[...]
-    all_single[f] = single[...]
 
     for step in range(1, nf):
         for copy in greens(step):
@@ -113,8 +122,21 @@
             real = real + (first[0] + second[0])
             imag = imag + (first[1] + second[1])
         for part, value in enumerate((real, imag)):
-            bubble[part, w] = jnp.dot(value * factor, pick, precision=lax.Precision.HIGHEST,
-                                      preferred_element_type=jnp.float32)
+            values[part * items + w * sites_here:part * items + (w + 1) * sites_here] = value * factor
+
+    whole = values[...]
+    high = whole.astype(jnp.bfloat16)
+    rest = whole - high.astype(jnp.float32)
+    middle = rest.astype(jnp.bfloat16)
+    low = (rest - middle.astype(jnp.float32)).astype(jnp.bfloat16)
+    spread = jnp.dot(jnp.concatenate([high, middle, low], axis=0), pick,
+                     preferred_element_type=jnp.float32)
+    total = 2 * items
+    spread = (spread[2 * total:] + spread[total:2 * total]) + spread[:total]
+    for part in range(2):
+        for w in range(local):
+            top = part * items + w * sites_here
+            bubble[part, w] = spread[top:top + sites_here]
 
     def own(i):
         return pltpu.make_async_copy(send.at[i, b], land.at[i, b], own_sem.at[i])
@@ -212,6 +234,7 @@
 def body(nf, nb, gamma, green, single, bond_site, causal_mask, site_perm):
     _, local, sites_here, order, _ = gamma.shape
     sites = green.shape[-1]
+    blocks = causal_mask.shape[-1]
     rows = order // nb
     seg = nb * sites_here
     items = local * sites_here
@@ -221,11 +244,16 @@
     return pl.pallas_call(
         functools.partial(kernel, nf, nb),
         out_shape=pltpu.VMEM((2, local, rows, seg, order), jnp.bfloat16),
-        in_specs=[pl.BlockSpec(memory_space=pl.ANY), vmem, vmem, vmem, pl.BlockSpec(memory_space=pltpu.SMEM), vmem],
+        in_specs=[pl.BlockSpec(memory_space=pl.ANY)] * 6,
         out_specs=vmem,
         scratch_shapes=[
             pltpu.VMEM((items, 2, order, order), jnp.bfloat16),
             dma((items,)),
+            pltpu.VMEM((order,), jnp.int32),
+            pltpu.SMEM((blocks, local, blocks), jnp.int32),
+            pltpu.VMEM((order,), jnp.int32),
+            pltpu.VMEM((2 * items, sites), jnp.float32),
+            dma((5,)),
             pltpu.VMEM((nf, 2, local, sites_here, sites), jnp.float32),
             pltpu.VMEM((nf, 2, local, sites_here, sites), jnp.float32),
             pltpu.VMEM((2, local, sites_here, order), jnp.float32),

time: 119 us -> 118 us (level)
  no operation moved by 1% of the time
where the time goes in v5:
time: 118 us; the launch traced here: 117 us
  Pallas kernels  115 us (97%)
  local copies, waits for them, and re-layouts  2.19 us (2%)
    pallas_call x1, Pallas kernels, body(): pl.pallas_call(functools.partial(kernel, nf, nb), out_shape=pltpu.VMEM((2...  115 us

profile of v5, /device:TPU:0, one launch (start us, length us, event | category | flops | bytes accessed | tf_op | source)
XLA Modules:
  0.0 117.4 jit_solution(17366906050322587791)
XLA Ops:
  0.0 115.2 %flow_exchange.1 = bf16[2,2,48,32,384]{4,3,2,1,0:T(8,128)(2,1)S(1)} custom-call(bf16[2,2,4,384,384]{4,3,2,1,0:T(8,128)(2,1)} %gamma_hbm.1, f32[2,2,4,256]{3,2,1,0:T(4,128)} %green.1, f32[2,2,4,256]{3,2,1,0:T(4,128)} %single.1, s32[384]{0:T(512)} %bond_hbm.1, s32[3,2,3]{2,1,0:T(2,128)} %bitcast.1, s32[384]{0:T(512)} %perm_hbm.1), custom_call_target="tpu_custom_call" | custom-call | tf_op jit(solution)/shard_map/flow_exchange/pallas_call | solution.py:244
  115.2 2.2 %copy.8 = bf16[2,2,48,32,384]{4,3,2,1,0:T(8,128)(2,1)} copy(bf16[2,2,48,32,384]{4,3,2,1,0:T(8,128)(2,1)S(1)} %flow_exchange.1) | data formatting | bytes 9437184

commit v6 on v5

--- a/solution.py
+++ b/solution.py
@@ -45,6 +45,8 @@
     count = local * nf
     seg = nb * sites_here
     items = local * sites_here
+    groups, deep = stage.shape[3], seg // stage.shape[3]
+    per = nb // groups
     f = lax.axis_index("freq")
     b = lax.axis_index("bond")
 
@@ -198,8 +200,18 @@
         for part in range(2):
             block = land[i, src, part].astype(jnp.float32)
             for c in range(order // LANES):
-                stage[w, part, c, pl.ds(src * sites_here + s, rows, stride=seg), :] = (
+                stage[w, part, c, src // per, pl.ds(lax.rem(src, per) * sites_here + s, rows, stride=deep), :] = (
                     block[:, c * LANES:(c + 1) * LANES])
+
+    def finish(i, group):
+        @pl.when(lax.rem(i, sites_here) == sites_here - 1)
+        def _():
+            w = i // sites_here
+            place = pl.ds(pl.multiple_of(group * deep, deep), deep)
+            for part in range(2):
+                for c in range(order // LANES):
+                    out[part, w, :, place, c * LANES:(c + 1) * LANES] = (
+                        stage[w, part, c, group].reshape(rows, deep, LANES).astype(jnp.bfloat16))
 
     def receive(i):
         own(i).wait()
@@ -208,14 +220,8 @@
             copy = outgoing(i, step)
             copy.wait_recv()
             arrange(i, origin(b, step, nb))
-
-        @pl.when(lax.rem(i, sites_here) == sites_here - 1)
-        def _():
-            w = i // sites_here
-            for part in range(2):
-                for c in range(order // LANES):
-                    out[part, w, :, :, c * LANES:(c + 1) * LANES] = (
-                        stage[w, part, c].reshape(rows, seg, LANES).astype(jnp.bfloat16))
+            if (step + 1) % per == 0:
+                finish(i, origin(b, step, nb) // per)
 
     def receive_last(i, carry):
         receive(i)
@@ -238,6 +244,7 @@
     rows = order // nb
     seg = nb * sites_here
     items = local * sites_here
+    deep = 8 if sites_here < 8 else sites_here
     result_bytes = 2 * local * rows * seg * order * 2
     vmem = pl.BlockSpec(memory_space=pltpu.VMEM)
     dma = pltpu.SemaphoreType.DMA
@@ -261,7 +268,7 @@
             pltpu.VMEM((order, order), jnp.bfloat16),
             pltpu.VMEM((items, nb, 2, rows, order), jnp.bfloat16),
             pltpu.VMEM((items, nb, 2, rows, order), jnp.bfloat16),
-            pltpu.VMEM((local, 2, order // LANES, rows * seg, LANES), jnp.float32),
+            pltpu.VMEM((local, 2, order // LANES, seg // deep, rows * deep, LANES), jnp.float32),
             dma((nf,)), dma((nf,)), dma((nf,)), dma((nf,)),
             dma((items, nb)), dma((items, nb)), dma((items,)),
         ],

time: 118 us -> 117 us (level)
  no operation moved by 1% of the time
where the time goes in v6:
time: 117 us
  Pallas kernels  115 us (98%)
  local copies, waits for them, and re-layouts  2.19 us (2%)
    pallas_call x1, Pallas kernels, body(): pl.pallas_call(functools.partial(kernel, nf, nb), out_shape=pltpu.VMEM((2...  115 us

profile of v6, /device:TPU:0, one launch (start us, length us, event | category | flops | bytes accessed | tf_op | source)
XLA Modules:
  0.0 116.8 jit_solution(15806028303964034799)
XLA Ops:
  0.0 114.6 %flow_exchange.1 = bf16[2,2,48,32,384]{4,3,2,1,0:T(8,128)(2,1)S(1)} custom-call(bf16[2,2,4,384,384]{4,3,2,1,0:T(8,128)(2,1)} %gamma_hbm.1, f32[2,2,4,256]{3,2,1,0:T(4,128)} %green.1, f32[2,2,4,256]{3,2,1,0:T(4,128)} %single.1, s32[384]{0:T(512)} %bond_hbm.1, s32[3,2,3]{2,1,0:T(2,128)} %bitcast.1, s32[384]{0:T(512)} %perm_hbm.1), custom_call_target="tpu_custom_call" | custom-call | tf_op jit(solution)/shard_map/flow_exchange/pallas_call | solution.py:251
  114.6 2.2 %copy.8 = bf16[2,2,48,32,384]{4,3,2,1,0:T(8,128)(2,1)} copy(bf16[2,2,48,32,384]{4,3,2,1,0:T(8,128)(2,1)S(1)} %flow_exchange.1) | data formatting | bytes 9437184
